TPU v7x, 32 devices: a whole 2x2x4 slice. The times are simulated.
32 devices in a mesh: req: 8 (over z, y), tp: 4 (over x, core).
Axes of the slice: x: 2, y: 2, z: 4, core: 2. Of those that a mesh axis runs over, the one named last changes fastest.
Arguments:
- tokens: bfloat16 [4096, 2048], P('req')
- token_request_number: int32 [8, 512], P('req'), may hold values from 0 to 7, never falling along the last dimension, each value on 1 to 256 neighbouring positions
- request_adapter_position: int32 [8, 8], P('req'), may hold values from 0 to 15
- adapters_in_use: int32 [16], replicated, may hold values from 0 to 15, as said below
- adapter_storage_slot: int32 [16], replicated, may hold values from 0 to 15, each once
- input_norm_gain: bfloat16 [2048], replicated, may hold values from 0.5 to 1.5
- query_weight: bfloat16 [2048, 2048], P('req', 'tp')
- key_weight: bfloat16 [2048, 2048], P('req', 'tp')
- value_weight: bfloat16 [2048, 2048], P('req', 'tp'), may hold values from -0.125 to 0.125
- output_weight: bfloat16 [2048, 2048], P('tp', 'req'), may hold values from -0.125 to 0.125
- adapter_down_weight: bfloat16 [16, 2, 16, 2048], P('req'), may hold values from -0.125 to 0.125
- adapter_up_weight: bfloat16 [16, 2, 16, 2048], P('req', None, None, 'tp'), may hold values from -0.75 to 0.75
Outputs:
- layer_out: bfloat16 [4096, 2048], P('req', 'tp')
Inputs may be any that keep to these rules, and one draw needn't show every extreme that they name: `adapters_in_use`: 16 different adapter numbers; 0 and 15 are always among them. `token_request_number`: the 512 tokens of each index of req form exactly 8 requests in order, each of 1 to 256 tokens, and one of exactly 256.
All inputs are finite; a program needn't handle non-finite values.
Results may differ from a plain program's by a relative error of at most 0.01.
Values may be sent and summed in bfloat16 or wider, within the bound.
A program may use at most 64 MiB of HBM per device.

v0:
```python
import jax
import jax.numpy as jnp
from jax import lax
from jax.sharding import PartitionSpec as P

HEAD_WIDTH = 64
norm_eps = 1e-05
rope_base = 130000.0
adapter_scale = 2.0


def fetch_adapters(down_part, up_part, active_slots, request_adapters, req_total):
    slot_total = down_part.shape[0]
    stored = jnp.concatenate([down_part, up_part], axis=1)
    split = down_part.shape[1]
    if slot_total * req_total <= 2 * active_slots.shape[0]:
        fetched = lax.all_gather(stored, "req", axis=0, tiled=True)
        places = active_slots[request_adapters]
    else:
        own = active_slots // slot_total == lax.axis_index("req")
        rows = jnp.where(
            own[:, None],
            jnp.take(stored, active_slots % slot_total, axis=0),
            jnp.zeros((), stored.dtype),
        )
        fetched = lax.psum(rows, "req")
        places = request_adapters
    return (fetched[:, :split], fetched[:, split:], places)


def positions_of(segment):
    ordinal = jnp.arange(segment.shape[0], dtype=jnp.int32)
    starts = jnp.concatenate([jnp.ones((1,), jnp.bool_), segment[1:] != segment[:-1]])
    segment_start = lax.cummax(jnp.where(starts, ordinal, jnp.zeros_like(ordinal)), axis=0)
    return ordinal - segment_start


def apply_rotation(values, token_positions):
    half_dim = HEAD_WIDTH // 2
    frequency = rope_base ** (-(jnp.arange(half_dim, dtype=jnp.float32) * 2.0 / HEAD_WIDTH))
    angles = token_positions.astype(jnp.float32)[:, None] * frequency[None, :]
    cosine = jnp.cos(angles)[:, None, :]
    sine_part = jnp.sin(angles)[:, None, :]
    first_half = values[..., :half_dim]
    second_half = values[..., half_dim:]
    return jnp.concatenate(
        [
            first_half * cosine - second_half * sine_part,
            second_half * cosine + first_half * sine_part,
        ],
        axis=-1,
    )


def attend(query_per_head, key_heads, value_per_head, segment):
    scores = (
        jnp.einsum("qhd,khd->hqk", query_per_head, key_heads, preferred_element_type=jnp.float32)
        * 0.125
    )
    ordinal = jnp.arange(segment.shape[0], dtype=jnp.int32)
    allowed = (segment[:, None] == segment[None, :]) & (ordinal[None, :] <= ordinal[:, None])
    scores = jnp.where(allowed[None], scores, jnp.float32(-1e30))
    row_peak = jnp.max(scores, axis=-1, keepdims=True)
    exponent = jnp.where(allowed[None], jnp.exp(scores - row_peak), jnp.float32(0.0))
    weights = (exponent / jnp.sum(exponent, axis=-1, keepdims=True)).astype(jnp.bfloat16)
    return jnp.einsum(
        "hqk,khd->qhd", weights, value_per_head, preferred_element_type=jnp.float32
    ).astype(jnp.bfloat16)


def local(
    tokens,
    token_request_number,
    request_adapter_position,
    adapters_in_use,
    adapter_storage_slot,
    input_norm_gain,
    query_weight,
    key_weight,
    value_weight,
    output_weight,
    adapter_down_weight,
    adapter_up_weight,
):
    row_total, model_width = tokens.shape
    local_width = query_weight.shape[1]
    reduced_rows = adapter_down_weight.shape[2]
    active_count = adapters_in_use.shape[0]
    slot_total = adapter_down_weight.shape[0]
    segment = token_request_number[0]
    request_adapters = request_adapter_position[0]
    tp_total = lax.axis_size("tp")
    req_total = lax.axis_size("req")
    part_rows = reduced_rows // tp_total
    down_part = lax.dynamic_slice_in_dim(
        adapter_down_weight, lax.axis_index("tp") * part_rows, part_rows, 2
    ).reshape(slot_total, 2 * part_rows * model_width)
    up_part = adapter_up_weight.reshape(slot_total, 2 * reduced_rows * local_width)
    down_all, up_all, request_places = fetch_adapters(
        down_part,
        up_part,
        jnp.take(adapter_storage_slot, adapters_in_use, axis=0),
        request_adapters,
        req_total,
    )
    place_total = down_all.shape[0]
    floats = tokens.astype(jnp.float32)
    normed = (
        floats
        * lax.rsqrt(jnp.mean(floats * floats, axis=-1, keepdims=True) + norm_eps)
        * input_norm_gain.astype(jnp.float32)
    ).astype(jnp.bfloat16)
    query_plain = jnp.dot(
        normed,
        lax.all_gather(query_weight, "req", axis=0, tiled=True),
        preferred_element_type=jnp.float32,
    )
    key_base = jnp.dot(
        normed,
        lax.all_gather(key_weight, "req", axis=0, tiled=True),
        preferred_element_type=jnp.float32,
    )
    value_plain = jnp.dot(
        normed,
        lax.all_gather(value_weight, "req", axis=0, tiled=True),
        preferred_element_type=jnp.float32,
    )
    request_total = request_adapters.shape[0]
    member = segment[:, None] == jnp.arange(request_total, dtype=jnp.int32)[None, :]
    token_place = jnp.sum(
        jnp.where(member, request_places[None, :], jnp.zeros_like(request_places)[None, :]), axis=1
    )
    share = 2 * part_rows
    shrunk_all = lax.dot_general(
        normed,
        down_all.reshape(place_total * share, model_width),
        (((1,), (1,)), ((), ())),
        preferred_element_type=jnp.float32,
    ).astype(jnp.bfloat16)
    column = jnp.arange(place_total * share, dtype=jnp.int32)
    kept = jnp.where(
        token_place[:, None] == (column // share)[None, :], shrunk_all, jnp.zeros((), jnp.bfloat16)
    )
    fold = (column % share)[:, None] == jnp.arange(share, dtype=jnp.int32)[None, :]
    shrunk_part = jnp.dot(
        kept, fold.astype(jnp.bfloat16), preferred_element_type=jnp.float32
    ).astype(jnp.bfloat16)
    shrunk = lax.all_gather(shrunk_part, "tp", axis=1, tiled=True)
    source = jnp.arange(tp_total * share, dtype=jnp.int32)
    source_kind = source % share // part_rows
    source_rank = source // share * part_rows + source % part_rows
    target = jnp.arange(place_total * reduced_rows, dtype=jnp.int32)
    mine = token_place[:, None] == (target // reduced_rows)[None, :]
    up_all = up_all.reshape(place_total, 2, reduced_rows, local_width)

    def change_of(kind):
        spread_map = (source_kind == kind)[:, None] & (
            source_rank[:, None] == (target % reduced_rows)[None, :]
        )
        spread = jnp.dot(
            shrunk, spread_map.astype(jnp.bfloat16), preferred_element_type=jnp.float32
        ).astype(jnp.bfloat16)
        spread = jnp.where(mine, spread, jnp.zeros((), jnp.bfloat16))
        return jnp.dot(
            spread,
            up_all[:, kind].reshape(place_total * reduced_rows, local_width),
            preferred_element_type=jnp.float32,
        )

    query_change = change_of(0)
    value_change = change_of(1)
    head_total = local_width // HEAD_WIDTH
    token_positions = positions_of(segment)
    query_per_head = apply_rotation(
        (query_plain + adapter_scale * query_change).reshape(row_total, head_total, HEAD_WIDTH),
        token_positions,
    ).astype(jnp.bfloat16)
    key_heads = apply_rotation(
        key_base.reshape(row_total, head_total, HEAD_WIDTH), token_positions
    ).astype(jnp.bfloat16)
    value_per_head = (
        (value_plain + adapter_scale * value_change)
        .astype(jnp.bfloat16)
        .reshape(row_total, head_total, HEAD_WIDTH)
    )
    attended = attend(query_per_head, key_heads, value_per_head, segment).reshape(
        row_total, local_width
    )
    partial_out = jnp.dot(
        attended,
        lax.all_gather(output_weight, "req", axis=1, tiled=True),
        preferred_element_type=jnp.float32,
    )
    summed = lax.psum_scatter(
        partial_out.astype(jnp.bfloat16), "tp", scatter_dimension=1, tiled=True
    ).astype(jnp.float32)
    share_width = summed.shape[1]
    residual_part = lax.dynamic_slice_in_dim(
        tokens, lax.axis_index("tp") * share_width, share_width, 1
    )
    return (summed + residual_part.astype(jnp.float32)).astype(jnp.bfloat16)


def solution(mesh):
    in_specs = (
        P("req", None),
        P("req", None),
        P("req", None),
        P(),
        P(),
        P(),
        P("req", "tp"),
        P("req", "tp"),
        P("req", "tp"),
        P("tp", "req"),
        P("req", None, None, None),
        P("req", None, None, "tp"),
    )
    out_specs = P("req", "tp")
    return jax.shard_map(local, mesh=mesh, in_specs=in_specs, out_specs=out_specs, check_vma=False)
```

profile of v0, /device:TPU:0, one launch (start us, length us, event | category | flops | bytes accessed | tf_op | source)
XLA Modules:
  0.0 296.7 jit_solution(14154784594400048160)
XLA Ops:
  6.5 0.0 all-gather.15.cloned.1.call-start
  6.6 1.0 copy.18
  7.7 0.1 reshape.292
  7.7 0.8 maximum_bitcast_fusion
  8.5 0.0 all-gather.7.cloned.1.call-start
  8.6 0.7 all-gather.7.cloned.1.call-update
  9.3 0.0 all-gather.9.cloned.1.call-start
  9.3 0.7 all-gather.9.cloned.1.call-update
  10.1 0.5 all-gather.11.cloned.1.call-update
  10.6 0.5 all-gather.13.cloned.1.call-update
  11.2 0.0 reduce-scatter.2.cloned.1.call-start
  11.3 0.7 convert_element_type.59
  12.0 2.1 fusion.2
  14.1 0.7 compare_select_fusion.1
  14.8 0.7 gather_fusion
  15.5 0.1 compare_reduce_fusion
  15.6 0.9 fusion.18
  16.5 0.6 gather_fusion.1
  17.1 0.1 select_reduce_fusion
  17.2 0.1 add_select_fusion
  17.3 0.3 reduce-window.9
  17.6 0.1 slice.46
  17.7 0.1 slice_reduce_fusion
  17.8 0.1 fusion.47
  17.9 0.9 multiply_cosine_fusion
  18.9 33.5 %all-gather.15.cloned.1.call-done = bf16[8,2,32768]{2,1,0:T(2,128)(2,1)} async-done(((bf16[1,2,32768]{2,1,0:T(2,128)(2,1)}), bf16[8,2,32768]{2,1,0:T(2,128)(2,1)}) %all-gather.15.cloned.1.call-update) | async-done | bytes 1048592 | tf_op jit(solution)/shard_map/all_gather | solution.py:17
  52.4 1.5 reshape.319
  53.9 0.9 fusion.70
  54.7 0.2 copy.19
  54.9 0.9 fusion.71
  55.8 1.3 reshape.294
  57.0 0.9 fusion.17
  58.0 5.4 %all_gather.20 = bf16[512,32]{0,1:T(8,128)(2,1)S(1)} all-gather(bf16[512,8]{0,1:T(8,128)(2,1)S(1)} %fusion.17), channel_id=1, replica_groups=mesh['req'=8,'tp'=4] {'tp'}, dimensions={1}, use_global_device_ids=true | all-gather | bytes 40960 | tf_op jit(solution)/shard_map/all_gather | solution.py:148
  63.4 39.2 %all-gather.7.cloned.1.call-done = bf16[2048,512]{1,0:T(8,128)(2,1)} async-done(((bf16[256,512]{1,0:T(8,128)(2,1)}), bf16[2048,512]{1,0:T(8,128)(2,1)}) %all-gather.7.cloned.1.call-update) | async-done | bytes 2097168 | tf_op jit(solution)/shard_map/all_gather | solution.py:125
  102.6 3.0 %fusion.68 = f32[512,512]{0,1:T(8,128)S(1)} fusion(bf16[2048,512]{1,0:T(8,128)(2,1)} %all-gather.7.cloned.1.call-done, bf16[512,2048]{1,0:T(8,128)(2,1)S(1)} %copy-done.2, f32[2048]{0:T(1024)S(1)} %convert_element_type.59, f32[512]{0:T(512)S(1)} %add_rsqrt_fusion), kind=kOutput, calls=%fused_computation.120 | convolution fusion | flops 1077936128 | bytes 5253120 | tf_op jit(solution)/shard_map/dot_general | solution.py:123
  105.6 2.3 fusion.12
  107.9 44.7 %all-gather.9.cloned.1.call-done = bf16[2048,512]{1,0:T(8,128)(2,1)} async-done(((bf16[256,512]{1,0:T(8,128)(2,1)}), bf16[2048,512]{1,0:T(8,128)(2,1)}) %all-gather.9.cloned.1.call-update) | async-done | bytes 2097168 | tf_op jit(solution)/shard_map/all_gather | solution.py:115
  152.5 3.9 %fusion.64 = f32[512,512]{0,1:T(8,128)} fusion(bf16[2048,512]{1,0:T(8,128)(2,1)} %all-gather.9.cloned.1.call-done, bf16[512,2048]{1,0:T(8,128)(2,1)S(1)} %copy-done.2, f32[2048]{0:T(1024)S(1)} %convert_element_type.59, f32[512]{0:T(512)S(1)} %add_rsqrt_fusion), kind=kOutput, calls=%fused_computation.119 | convolution fusion | flops 1077936128 | bytes 5253120 | tf_op jit(solution)/shard_map/dot_general | solution.py:113
  156.5 1.9 fusion.9
  158.4 44.0 %all-gather.11.cloned.1.call-done = bf16[2048,512]{1,0:T(8,128)(2,1)} async-done(((bf16[256,512]{1,0:T(8,128)(2,1)}), bf16[2048,512]{1,0:T(8,128)(2,1)}) %all-gather.11.cloned.1.call-update) | async-done | bytes 2097168 | tf_op jit(solution)/shard_map/all_gather | solution.py:120
  202.3 3.0 %fusion.62 = f32[512,512]{0,1:T(8,128)S(1)} fusion(bf16[2048,512]{1,0:T(8,128)(2,1)} %all-gather.11.cloned.1.call-done, bf16[512,2048]{1,0:T(8,128)(2,1)S(1)} %copy-done.2, f32[2048]{0:T(1024)S(1)} %convert_element_type.59, f32[512]{0:T(512)S(1)} %add_rsqrt_fusion), kind=kOutput, calls=%fused_computation.118 | convolution fusion | flops 1077936128 | bytes 5253120 | tf_op jit(solution)/shard_map/dot_general | solution.py:118
  205.4 1.3 subtract_convert_fusion.1
  206.7 8.2 %fusion.72 = (f32[8,512]{1,0:T(8,128)S(1)}, f32[8,512,512]{1,2,0:T(8,128)}) fusion(pred[512,512]{0,1:T(8,128)(4,1)} %fusion.18, bf16[512,8,32]{0,2,1:T(8,128)(2,1)} %get-tuple-element.13, bf16[512,8,32]{0,2,1:T(8,128)(2,1)} %get-tuple-element.14, bf16[512,8,32]{0,2,1:T(8,128)(2,1)} %get-tuple-element.6, bf16[512,8,32]{0,2,1:T(8,128)(2,1)} %get-tuple-element.5), kind=kOutput, calls=%fused_computation.123 | convolution fusion | flops 281018880 | bytes 9715712 | tf_op jit(solution)/shard_map/sub | solution.py:64
  214.9 4.3 %fusion.11 = bf16[8,64,512]{2,1,0:T(8,128)(2,1)S(1)} fusion(bf16[512,8,64]{0,2,1:T(8,128)(2,1)S(1)} %bitcast.46, f32[8,512,512]{1,2,0:T(8,128)} %get-tuple-element.18, f32[8,512]{1,0:T(8,128)S(1)} %get-tuple-element.17), kind=kOutput, calls=%fused_computation.21 | convolution fusion | flops 272891904 | bytes 9453568 | tf_op jit(solution)/shard_map/hqk,khd->qhd/dot_general | solution.py:66
  219.2 34.7 %all-gather.13.cloned.1.call-done = bf16[512,2048]{1,0:T(8,128)(2,1)} async-done(((bf16[512,256]{1,0:T(8,128)(2,1)}), bf16[512,2048]{1,0:T(8,128)(2,1)}) %all-gather.13.cloned.1.call-update) | async-done | bytes 2097168 | tf_op jit(solution)/shard_map/all_gather | solution.py:191
  253.8 4.2 %convolution_convert_fusion = bf16[512,2048]{1,0:T(8,128)(2,1)} fusion(bf16[512,512]{0,1:T(8,128)(2,1)S(1)} %bitcast.51, bf16[512,2048]{1,0:T(8,128)(2,1)} %all-gather.13.cloned.1.call-done), kind=kOutput, calls=%fused_computation.16 | convolution fusion | flops 1074790400 | bytes 4718592 | tf_op jit(solution)/shard_map/dot_general | solution.py:189
  258.1 29.8 %reduce-scatter.2.cloned.1.call-done = bf16[512,512]{1,0:T(8,128)(2,1)} async-done(((bf16[512,2048]{1,0:T(8,128)(2,1)}), bf16[512,512]{1,0:T(8,128)(2,1)}) %reduce-scatter.2.cloned.1.call-update) | async-done | bytes 524304 | tf_op jit(solution)/shard_map/reduce_scatter | solution.py:194
  287.8 2.0 add_convert_fusion
  (33 shorter events, 0.3 us)
Async XLA Ops:
  6.5 1.1 copy-start
  6.5 8.9 %copy-start.6 = (s32[16]{0:T(128)S(1)}, s32[16]{0:T(128)}, u32[]{:S(2)}) copy-start(s32[16]{0:T(128)} %param.15) | copy-start | bytes 196
  6.5 8.2 %copy-start.1 = (s32[16]{0:T(128)S(1)}, s32[16]{0:T(128)}, u32[]{:S(2)}) copy-start(s32[16]{0:T(128)} %param.16) | copy-start | bytes 196
  6.5 8.9 %copy-start.7 = (s32[1,8]{1,0:T(1,128)S(1)}, s32[1,8]{1,0:T(1,128)}, u32[]{:S(2)}) copy-start(s32[1,8]{1,0:T(1,128)} %param.14) | copy-start | bytes 100
  6.5 8.9 %copy-start.5 = (s32[1,512]{1,0:T(1,128)S(1)}, s32[1,512]{1,0:T(1,128)}, u32[]{:S(2)}) copy-start(s32[1,512]{1,0:T(1,128)} %param.13) | copy-start | bytes 6148
  6.5 45.8 %all-gather.15.cloned.1.call-start = ((), (), s32[]{:S(2)}) async-start(), calls=%async_computation.6 | async-start | bytes 1179648 | tf_op jit(solution)/shard_map/all_gather | solution.py:17
  8.5 94.1 %all-gather.7.cloned.1.call-start = ((), (), s32[]{:S(2)}) async-start(), calls=%async_computation.1 | async-start | bytes 2359296 | tf_op jit(solution)/shard_map/all_gather | solution.py:125
  9.3 143.3 %all-gather.9.cloned.1.call-start = ((), (), s32[]{:S(2)}) async-start(), calls=%async_computation.2 | async-start | bytes 2359296 | tf_op jit(solution)/shard_map/all_gather | solution.py:115
  10.0 192.3 %all-gather.11.cloned.1.call-start = ((), (), s32[]{:S(2)}) async-start(), calls=%async_computation.3 | async-start | bytes 2359296 | tf_op jit(solution)/shard_map/all_gather | solution.py:120
  10.6 243.2 %all-gather.13.cloned.1.call-start = ((), (), s32[]{:S(2)}) async-start(), calls=%async_computation.4 | async-start | bytes 2359296 | tf_op jit(solution)/shard_map/all_gather | solution.py:191
  11.2 276.6 %reduce-scatter.2.cloned.1.call-start = ((), (), s32[]{:S(2)}) async-start(), calls=%async_computation.5 | async-start | bytes 2621440 | tf_op jit(solution)/shard_map/reduce_scatter | solution.py:194
  15.4 41.6 %copy-start.2 = (bf16[512,2048]{1,0:T(8,128)(2,1)S(1)}, bf16[512,2048]{1,0:T(8,128)(2,1)}, u32[]{:S(2)}) copy-start(bf16[512,2048]{1,0:T(8,128)(2,1)} %param.12) | copy-start | bytes 6291460
  202.3 3.0 %copy-start.4 = (f32[512,32]{0,1:T(8,128)S(1)}, f32[512,32]{0,1:T(8,128)}, u32[]{:S(2)}) copy-start(f32[512,32]{0,1:T(8,128)} %get-tuple-element.16) | copy-start | bytes 196612
  206.7 8.2 %copy-start.3 = (bf16[512,512]{0,1:T(8,128)(2,1)S(1)}, bf16[512,512]{0,1:T(8,128)(2,1)}, u32[]{:S(2)}) copy-start(bf16[512,512]{0,1:T(8,128)(2,1)} %fusion.12) | copy-start | bytes 1572868
Sparse Core Ops, SparseCore 0:
  9.5 42.8 all-gather.14
  54.5 48.0 all-gather.6
  104.7 47.7 all-gather.8
  154.5 47.7 all-gather.10
  204.2 49.5 all-gather.12
  258.2 29.5 reduce-scatter.1
where the time goes:
time: 297 us
  waiting for transfers between devices  228 us (77%)
  matrix products  31.7 us (11%)
  between operations  13.7 us (5%)
  other arithmetic  10.1 us (3%)
  local copies, waits for them, and re-layouts  7.27 us (2%)
  blocking collectives  5.39 us (2%)
    all_gather x1, waiting for transfers between devices, local(): lax.all_gather(query_weight, 'req', axis=0, tiled=True)  44.7 us
    all_gather x1, waiting for transfers between devices, local(): lax.all_gather(key_weight, 'req', axis=0, tiled=True)  44 us
    all_gather x1, waiting for transfers between devices, local(): lax.all_gather(value_weight, 'req', axis=0, tiled=True)  39.2 us
    all_gather x1, waiting for transfers between devices, local(): lax.all_gather(output_weight, 'req', axis=1, tiled=True)  34.7 us
    all_gather x1, waiting for transfers between devices, fetch_adapters(): fetched = lax.all_gather(stored, 'req', axis=0, tiled=True)  33.5 us
    reduce_scatter x1, waiting for transfers between devices, local(): lax.psum_scatter(partial_out.astype(jnp.bfloat16), 'tp', scatter_dimensio...  29.8 us
    sub x1, matrix products, attend(): scores - row_peak  8.2 us
  transfers between devices with their start and end apart: 6, of which 6 were waited for; matrix products, arithmetic and copies ran while one was open for 14% of the time, Pallas kernels for 0%

commit v1 on v0

--- a/solution.py
+++ b/solution.py
@@ -2,11 +2,46 @@
 import jax.numpy as jnp
 from jax import lax
 from jax.sharding import PartitionSpec as P
+from jax.lax import axis_index, axis_size, ppermute
 
 HEAD_WIDTH = 64
 norm_eps = 1e-05
 rope_base = 130000.0
 adapter_scale = 2.0
+
+
+def _load_spans(in_array, a_name):
+    local_out = axis_size(a_name)
+    block_last, ready, h_now = (local_out, axis_index(a_name), in_array.shape[0])
+    items = []
+    for u, j0 in enumerate(in_array.shape):
+        items.append(j0 * block_last if u == 0 else j0)
+    item_now = jnp.zeros(items, in_array.dtype)
+    step_out = lax.dynamic_update_slice_in_dim(item_now, in_array, ready * h_now, axis=0)
+    after = plain = in_array
+    ix = 1
+    while ix < block_last // 2 + 1:
+        grid = []
+        u = 0
+        while u < block_last:
+            grid.append((u, (u + 1) % block_last))
+            u += 1
+        after = ppermute(after, axis_name=a_name, perm=grid)
+        step_out = lax.dynamic_update_slice_in_dim(
+            step_out, after, (ready - ix) % block_last * h_now, axis=0
+        )
+        if 2 * ix < block_last:
+            stack_in = []
+            u = 0
+            while u < block_last:
+                stack_in.append((u, (u - 1) % block_last))
+                u += 1
+            plain = ppermute(plain, a_name, perm=stack_in)
+            step_out = lax.dynamic_update_slice_in_dim(
+                step_out, plain, (ready + ix) % block_last * h_now, axis=0
+            )
+        ix = ix + 1
+    return step_out
 
 
 def fetch_adapters(down_part, up_part, active_slots, request_adapters, req_total):
@@ -121,9 +156,7 @@
         preferred_element_type=jnp.float32,
     )
     value_plain = jnp.dot(
-        normed,
-        lax.all_gather(value_weight, "req", axis=0, tiled=True),
-        preferred_element_type=jnp.float32,
+        normed, _load_spans(value_weight, "req"), preferred_element_type=jnp.float32
     )
     request_total = request_adapters.shape[0]
     member = segment[:, None] == jnp.arange(request_total, dtype=jnp.int32)[None, :]

time: 297 us -> 264 us (0.89)
  waiting for transfers between devices: 228 us -> 170 us
  starting transfers between devices: 0.23 us -> 19.9 us
  local copies, waits for them, and re-layouts: 7.27 us -> 14.2 us
    all_gather x1 -> x0, waiting for transfers between devices: 39.2 us -> none  [local(): lax.all_gather(value_weight, 'req', axis=0, tiled=True)]
    all_gather x1, waiting for transfers between devices: 33.5 us -> 0.01 us  [fetch_adapters(): fetched = lax.all_gather(stored, 'req', axis=0, tiled=True)]
    ppermute x0 -> x7, waiting for transfers between devices: none -> 26.9 us  [the longest x4 24.4 us: _load_spans(): after = ppermute(after, axis_name=a_name, perm=grid)]
    ppermute x0 -> x7, starting transfers between devices: none -> 19.7 us  [the longest x4 10.1 us: _load_spans(): after = ppermute(after, axis_name=a_name, perm=grid)]
    all_gather x1, waiting for transfers between devices: 44.7 us -> 33.6 us  [local(): lax.all_gather(query_weight, 'req', axis=0, tiled=True)]
    dynamic_update_slice x0 -> x8, local copies, waits for them, and re-layouts: none -> 5.8 us  [the longest x4 2.91 us: _load_spans(): lax.dynamic_update_slice_in_dim(step_out, after, (ready - ix) % block_las...]
  transfers between devices with their start and end apart: 6 -> 12, of which waited for: 6 -> 10; matrix products, arithmetic and copies ran while one was open for 14% -> 17% of each run, Pallas kernels for 0% -> 0%
where the time goes in v1:
time: 264 us; the launch traced here: 263 us
  waiting for transfers between devices  170 us (64%)
  matrix products  31.7 us (12%)
  starting transfers between devices  19.9 us (8%)
  local copies, waits for them, and re-layouts  14.2 us (5%)
  between operations  13.5 us (5%)
  other arithmetic  7.84 us (3%)
  blocking collectives  5.38 us (2%)
    all_gather x1, waiting for transfers between devices, local(): lax.all_gather(key_weight, 'req', axis=0, tiled=True)  44.1 us
    all_gather x1, waiting for transfers between devices, local(): lax.all_gather(output_weight, 'req', axis=1, tiled=True)  34.7 us
    all_gather x1, waiting for transfers between devices, local(): lax.all_gather(query_weight, 'req', axis=0, tiled=True)  33.6 us
    reduce_scatter x1, waiting for transfers between devices, local(): lax.psum_scatter(partial_out.astype(jnp.bfloat16), 'tp', scatter_dimensio...  29.8 us
    ppermute x4, waiting for transfers between devices, _load_spans(): after = ppermute(after, axis_name=a_name, perm=grid)  24.4 us
    ppermute x4, starting transfers between devices, _load_spans(): after = ppermute(after, axis_name=a_name, perm=grid)  10.1 us
    ppermute x3, starting transfers between devices, _load_spans(): plain = ppermute(plain, a_name, perm=stack_in)  9.61 us
    sub x1, matrix products, attend(): scores - row_peak  8.19 us
  transfers between devices with their start and end apart: 12, of which 10 were waited for; matrix products, arithmetic and copies ran while one was open for 17% of the time, Pallas kernels for 0%

profile of v1, /device:TPU:0, one launch (start us, length us, event | category | flops | bytes accessed | tf_op | source)
XLA Modules:
  0.0 263.0 jit_solution(12286068557097191979)
XLA Ops:
  6.6 1.1 copy.18
  7.8 0.8 maximum_bitcast_fusion
  8.7 0.7 all-gather.6.cloned.1.call-update
  9.4 0.7 all-gather.8.cloned.1.call-update
  10.1 3.0 %collective-permute-start = (bf16[256,512]{1,0:T(8,128)(2,1)}, bf16[256,512]{1,0:T(8,128)(2,1)S(1)}, u32[]{:S(2)}, u32[]{:S(2)}) collective-permute-start(bf16[256,512]{1,0:T(8,128)(2,1)} %param.20), channel_id=1, source_target_pairs={{0,4},{4,8},{8,12},{12,16},{16,20},{20,24},{24,28},{28,0},{1,5},{5... | collective-permute-start | bytes 786440 | tf_op jit(solution)/shard_map/ppermute | solution.py:29
  13.2 3.1 %collective-permute-start.1 = (bf16[256,512]{1,0:T(8,128)(2,1)}, bf16[256,512]{1,0:T(8,128)(2,1)S(1)}, u32[]{:S(2)}, u32[]{:S(2)}) collective-permute-start(bf16[256,512]{1,0:T(8,128)(2,1)} %param.20), channel_id=1, source_target_pairs={{0,28},{4,0},{8,4},{12,8},{16,12},{20,16},{24,20},{28,24},{1,29},{... | collective-permute-start | bytes 786440 | tf_op jit(solution)/shard_map/ppermute | solution.py:39
  16.4 0.7 compare_select_fusion.1
  17.0 1.3 gather_fusion
  19.0 0.9 fusion.17
  20.6 0.9 multiply_cosine_fusion
  22.3 3.7 %collective-permute-done = bf16[256,512]{1,0:T(8,128)(2,1)S(1)} collective-permute-done((bf16[256,512]{1,0:T(8,128)(2,1)}, bf16[256,512]{1,0:T(8,128)(2,1)S(1)}, u32[]{:S(2)}, u32[]{:S(2)}) %collective-permute-start) | collective-permute-done | bytes 262176 | tf_op jit(solution)/shard_map/ppermute | solution.py:29
  26.1 2.4 collective-permute-start.2
  28.5 1.5 broadcast_in_dim.47
  29.9 0.7 constant_dynamic-update-slice_fusion.7
  30.6 3.0 %collective-permute-start.3 = (bf16[256,512]{1,0:T(8,128)(2,1)S(1)}, bf16[256,512]{1,0:T(8,128)(2,1)S(1)}, u32[]{:S(2)}, u32[]{:S(2)}) collective-permute-start(bf16[256,512]{1,0:T(8,128)(2,1)S(1)} %collective-permute-done.1), channel_id=1, source_target_pairs={{0,28},{4,0},{8,4},{12,8},{16,12},{20,16},{24,20},{28,24},{1,29},{... | collective-permute-start | bytes 786440 | tf_op jit(solution)/shard_map/ppermute | solution.py:39
  33.9 5.2 %collective-permute-done.2 = bf16[256,512]{1,0:T(8,128)(2,1)S(1)} collective-permute-done((bf16[256,512]{1,0:T(8,128)(2,1)S(1)}, bf16[256,512]{1,0:T(8,128)(2,1)S(1)}, u32[]{:S(2)}, u32[]{:S(2)}) %collective-permute-start.2) | collective-permute-done | bytes 262176 | tf_op jit(solution)/shard_map/ppermute | solution.py:29
  39.0 2.2 collective-permute-start.4
  41.2 0.7 constant_dynamic-update-slice_fusion.6
  41.9 0.7 constant_dynamic-update-slice_fusion.5
  43.0 3.5 %collective-permute-start.5 = (bf16[256,512]{1,0:T(8,128)(2,1)S(1)}, bf16[256,512]{1,0:T(8,128)(2,1)S(1)}, u32[]{:S(2)}, u32[]{:S(2)}) collective-permute-start(bf16[256,512]{1,0:T(8,128)(2,1)S(1)} %collective-permute-done.3), channel_id=1, source_target_pairs={{0,28},{4,0},{8,4},{12,8},{16,12},{20,16},{24,20},{28,24},{1,29},{... | collective-permute-start | bytes 786440 | tf_op jit(solution)/shard_map/ppermute | solution.py:39
  46.4 0.7 constant_dynamic-update-slice_fusion.4
  47.2 10.2 %collective-permute-done.4 = bf16[256,512]{1,0:T(8,128)(2,1)S(1)} collective-permute-done((bf16[256,512]{1,0:T(8,128)(2,1)S(1)}, bf16[256,512]{1,0:T(8,128)(2,1)S(1)}, u32[]{:S(2)}, u32[]{:S(2)}) %collective-permute-start.4) | collective-permute-done | bytes 262176 | tf_op jit(solution)/shard_map/ppermute | solution.py:29
  57.4 2.5 collective-permute-start.6
  59.9 0.7 constant_dynamic-update-slice_fusion.3
  60.6 0.7 constant_dynamic-update-slice_fusion.2
  61.4 2.2 collective-permute-done.5
  63.6 0.7 constant_dynamic-update-slice_fusion.1
  64.3 5.2 %collective-permute-done.6 = bf16[256,512]{1,0:T(8,128)(2,1)S(1)} collective-permute-done((bf16[256,512]{1,0:T(8,128)(2,1)S(1)}, bf16[256,512]{1,0:T(8,128)(2,1)S(1)}, u32[]{:S(2)}, u32[]{:S(2)}) %collective-permute-start.6) | collective-permute-done | bytes 262176 | tf_op jit(solution)/shard_map/ppermute | solution.py:29
  69.5 0.7 constant_dynamic-update-slice_fusion
  70.2 1.5 reshape.319
  71.7 0.9 fusion.68
  72.7 0.8 fusion.69
  73.9 1.0 fusion.16
  74.8 5.4 %all_gather.16 = bf16[512,32]{0,1:T(8,128)(2,1)S(1)} all-gather(bf16[512,8]{0,1:T(8,128)(2,1)S(1)} %fusion.16), channel_id=1, replica_groups=mesh['req'=8,'tp'=4] {'tp'}, dimensions={1}, use_global_device_ids=true | all-gather | bytes 40960 | tf_op jit(solution)/shard_map/all_gather | solution.py:181
  80.2 1.5 convolution_multiply_fusion.1
  81.7 3.8 %fusion.11 = bf16[512,512]{0,1:T(8,128)(2,1)} fusion(f32[512,512]{0,1:T(8,128)S(1)} %convolution_multiply_fusion.1, bf16[2048,512]{1,0:T(8,128)(2,1)} %constant_dynamic-update-slice_fusion, bf16[512,2048]{1,0:T(8,128)(2,1)S(1)} %copy-done.1, f32[2048]{0:T(1024)S(1)} %convert_element_type.59, f32[512]{0:T(512)S(1)} %add_rsqrt_fusion), kind=kOutput, calls=%fused_computation.22 | convolution fusion | flops 1078460416 | bytes 5777408 | tf_op jit(solution)/shard_map/dot_general | solution.py:158
  85.5 33.6 %all-gather.6.cloned.1.call-done = bf16[2048,512]{1,0:T(8,128)(2,1)} async-done(((bf16[256,512]{1,0:T(8,128)(2,1)}), bf16[2048,512]{1,0:T(8,128)(2,1)}) %all-gather.6.cloned.1.call-update) | async-done | bytes 2097168 | tf_op jit(solution)/shard_map/all_gather | solution.py:150
  119.1 3.9 %fusion.63 = f32[512,512]{0,1:T(8,128)} fusion(bf16[2048,512]{1,0:T(8,128)(2,1)} %all-gather.6.cloned.1.call-done, bf16[512,2048]{1,0:T(8,128)(2,1)S(1)} %copy-done.1, f32[2048]{0:T(1024)S(1)} %convert_element_type.59, f32[512]{0:T(512)S(1)} %add_rsqrt_fusion), kind=kOutput, calls=%fused_computation.127 | convolution fusion | flops 1077936128 | bytes 5253120 | tf_op jit(solution)/shard_map/dot_general | solution.py:148
  123.0 1.9 fusion.9
  124.9 44.1 %all-gather.8.cloned.1.call-done = bf16[2048,512]{1,0:T(8,128)(2,1)} async-done(((bf16[256,512]{1,0:T(8,128)(2,1)}), bf16[2048,512]{1,0:T(8,128)(2,1)}) %all-gather.8.cloned.1.call-update) | async-done | bytes 2097168 | tf_op jit(solution)/shard_map/all_gather | solution.py:155
  169.0 3.0 %fusion.61 = f32[512,512]{0,1:T(8,128)S(1)} fusion(bf16[2048,512]{1,0:T(8,128)(2,1)} %all-gather.8.cloned.1.call-done, bf16[512,2048]{1,0:T(8,128)(2,1)S(1)} %copy-done.1, f32[2048]{0:T(1024)S(1)} %convert_element_type.59, f32[512]{0:T(512)S(1)} %add_rsqrt_fusion), kind=kOutput, calls=%fused_computation.126 | convolution fusion | flops 1077936128 | bytes 5253120 | tf_op jit(solution)/shard_map/dot_general | solution.py:153
  172.0 1.3 subtract_convert_fusion.1
  173.3 8.2 %fusion.70 = (f32[8,512]{1,0:T(8,128)S(1)}, f32[8,512,512]{1,2,0:T(8,128)}) fusion(pred[512,512]{0,1:T(8,128)(4,1)} %fusion.17, bf16[512,8,32]{0,2,1:T(8,128)(2,1)} %get-tuple-element.13, bf16[512,8,32]{0,2,1:T(8,128)(2,1)} %get-tuple-element.14, bf16[512,8,32]{0,2,1:T(8,128)(2,1)} %get-tuple-element.6, bf16[512,8,32]{0,2,1:T(8,128)(2,1)} %get-tuple-element.5), kind=kOutput, calls=%fused_computation.130 | convolution fusion | flops 281018880 | bytes 9715712 | tf_op jit(solution)/shard_map/sub | solution.py:99
  181.5 4.2 %fusion.10 = bf16[8,64,512]{2,1,0:T(8,128)(2,1)S(1)} fusion(bf16[512,8,64]{0,2,1:T(8,128)(2,1)S(1)} %bitcast.50, f32[8,512,512]{1,2,0:T(8,128)} %get-tuple-element.18, f32[8,512]{1,0:T(8,128)S(1)} %get-tuple-element.17), kind=kOutput, calls=%fused_computation.21 | convolution fusion | flops 272891904 | bytes 9453568 | tf_op jit(solution)/shard_map/hqk,khd->qhd/dot_general | solution.py:101
  185.8 34.7 %all-gather.10.cloned.1.call-done = bf16[512,2048]{1,0:T(8,128)(2,1)} async-done(((bf16[512,256]{1,0:T(8,128)(2,1)}), bf16[512,2048]{1,0:T(8,128)(2,1)}) %all-gather.10.cloned.1.call-update) | async-done | bytes 2097168 | tf_op jit(solution)/shard_map/all_gather | solution.py:224
  220.5 4.2 %convolution_convert_fusion = bf16[512,2048]{1,0:T(8,128)(2,1)} fusion(bf16[512,512]{0,1:T(8,128)(2,1)S(1)} %bitcast.51, bf16[512,2048]{1,0:T(8,128)(2,1)} %all-gather.10.cloned.1.call-done), kind=kOutput, calls=%fused_computation.16 | convolution fusion | flops 1074790400 | bytes 4718592 | tf_op jit(solution)/shard_map/dot_general | solution.py:222
  224.7 29.8 %reduce-scatter.2.cloned.1.call-done = bf16[512,512]{1,0:T(8,128)(2,1)} async-done(((bf16[512,2048]{1,0:T(8,128)(2,1)}), bf16[512,512]{1,0:T(8,128)(2,1)}) %reduce-scatter.2.cloned.1.call-update) | async-done | bytes 524304 | tf_op jit(solution)/shard_map/reduce_scatter | solution.py:227
  254.5 2.0 add_convert_fusion
  (57 shorter events, 3.2 us)
Async XLA Ops:
  6.5 1.1 copy-start
  6.5 11.8 %copy-start.7 = (s32[16]{0:T(128)S(1)}, s32[16]{0:T(128)}, u32[]{:S(2)}) copy-start(s32[16]{0:T(128)} %param.15) | copy-start | bytes 196
  6.5 11.8 %copy-start.8 = (s32[1,8]{1,0:T(1,128)S(1)}, s32[1,8]{1,0:T(1,128)}, u32[]{:S(2)}) copy-start(s32[1,8]{1,0:T(1,128)} %param.14) | copy-start | bytes 100
  6.5 11.9 %copy-start.1 = (bf16[512,2048]{1,0:T(8,128)(2,1)S(1)}, bf16[512,2048]{1,0:T(8,128)(2,1)}, u32[]{:S(2)}) copy-start(bf16[512,2048]{1,0:T(8,128)(2,1)} %param.12) | copy-start | bytes 6291460
  6.5 63.7 %all-gather.12.cloned.1.call-start = ((), (), s32[]{:S(2)}) async-start(), calls=%async_computation.5 | async-start | bytes 1179648 | tf_op jit(solution)/shard_map/all_gather | solution.py:52
  6.6 12.3 %copy-start.5 = (s32[1,512]{1,0:T(1,128)S(1)}, s32[1,512]{1,0:T(1,128)}, u32[]{:S(2)}) copy-start(s32[1,512]{1,0:T(1,128)} %param.13) | copy-start | bytes 6148
  8.6 110.5 %all-gather.6.cloned.1.call-start = ((), (), s32[]{:S(2)}) async-start(), calls=%async_computation.1 | async-start | bytes 2359296 | tf_op jit(solution)/shard_map/all_gather | solution.py:150
  9.4 159.6 %all-gather.8.cloned.1.call-start = ((), (), s32[]{:S(2)}) async-start(), calls=%async_computation.2 | async-start | bytes 2359296 | tf_op jit(solution)/shard_map/all_gather | solution.py:155
  10.1 210.4 %all-gather.10.cloned.1.call-start = ((), (), s32[]{:S(2)}) async-start(), calls=%async_computation.3 | async-start | bytes 2359296 | tf_op jit(solution)/shard_map/all_gather | solution.py:224
  10.1 15.9 %collective-permute-start = (bf16[256,512]{1,0:T(8,128)(2,1)}, bf16[256,512]{1,0:T(8,128)(2,1)S(1)}, u32[]{:S(2)}, u32[]{:S(2)}) collective-permute-start(bf16[256,512]{1,0:T(8,128)(2,1)} %param.20), channel_id=1, source_target_pairs={{0,4},{4,8},{8,12},{12,16},{16,20},{20,24},{24,28},{28,0},{1,5},{5... | collective-permute-start | bytes 786440 | tf_op jit(solution)/shard_map/ppermute | solution.py:29
  13.2 17.5 %collective-permute-start.1 = (bf16[256,512]{1,0:T(8,128)(2,1)}, bf16[256,512]{1,0:T(8,128)(2,1)S(1)}, u32[]{:S(2)}, u32[]{:S(2)}) collective-permute-start(bf16[256,512]{1,0:T(8,128)(2,1)} %param.20), channel_id=1, source_target_pairs={{0,28},{4,0},{8,4},{12,8},{16,12},{20,16},{24,20},{28,24},{1,29},{... | collective-permute-start | bytes 786440 | tf_op jit(solution)/shard_map/ppermute | solution.py:39
  16.3 238.2 %reduce-scatter.2.cloned.1.call-start = ((), (), s32[]{:S(2)}) async-start(), calls=%async_computation.4 | async-start | bytes 2621440 | tf_op jit(solution)/shard_map/reduce_scatter | solution.py:227
  18.4 11.5 %copy-start.3 = (bf16[256,512]{1,0:T(8,128)(2,1)S(1)}, bf16[256,512]{1,0:T(8,128)(2,1)}, u32[]{:S(2)}) copy-start(bf16[256,512]{1,0:T(8,128)(2,1)} %param.20) | copy-start | bytes 786436
  18.9 14.9 %copy-start.6 = (bf16[2048]{0:T(1024)(128)(2,1)S(1)}, bf16[2048]{0:T(1024)(128)(2,1)}, u32[]{:S(2)}) copy-start(bf16[2048]{0:T(1024)(128)(2,1)} %param.17) | copy-start | bytes 12292
  26.1 13.0 %collective-permute-start.2 = (bf16[256,512]{1,0:T(8,128)(2,1)S(1)}, bf16[256,512]{1,0:T(8,128)(2,1)S(1)}, u32[]{:S(2)}, u32[]{:S(2)}) collective-permute-start(bf16[256,512]{1,0:T(8,128)(2,1)S(1)} %collective-permute-done), channel_id=1, source_target_pairs={{0,4},{4,8},{8,12},{12,16},{16,20},{20,24},{24,28},{28,0},{1,5},{5... | collective-permute-start | bytes 786440 | tf_op jit(solution)/shard_map/ppermute | solution.py:29
  30.6 12.3 %collective-permute-start.3 = (bf16[256,512]{1,0:T(8,128)(2,1)S(1)}, bf16[256,512]{1,0:T(8,128)(2,1)S(1)}, u32[]{:S(2)}, u32[]{:S(2)}) collective-permute-start(bf16[256,512]{1,0:T(8,128)(2,1)S(1)} %collective-permute-done.1), channel_id=1, source_target_pairs={{0,28},{4,0},{8,4},{12,8},{16,12},{20,16},{24,20},{28,24},{1,29},{... | collective-permute-start | bytes 786440 | tf_op jit(solution)/shard_map/ppermute | solution.py:39
  39.0 18.4 %collective-permute-start.4 = (bf16[256,512]{1,0:T(8,128)(2,1)S(1)}, bf16[256,512]{1,0:T(8,128)(2,1)S(1)}, u32[]{:S(2)}, u32[]{:S(2)}) collective-permute-start(bf16[256,512]{1,0:T(8,128)(2,1)S(1)} %collective-permute-done.2), channel_id=1, source_target_pairs={{0,4},{4,8},{8,12},{12,16},{16,20},{20,24},{24,28},{28,0},{1,5},{5... | collective-permute-start | bytes 786440 | tf_op jit(solution)/shard_map/ppermute | solution.py:29
  43.0 20.6 %collective-permute-start.5 = (bf16[256,512]{1,0:T(8,128)(2,1)S(1)}, bf16[256,512]{1,0:T(8,128)(2,1)S(1)}, u32[]{:S(2)}, u32[]{:S(2)}) collective-permute-start(bf16[256,512]{1,0:T(8,128)(2,1)S(1)} %collective-permute-done.3), channel_id=1, source_target_pairs={{0,28},{4,0},{8,4},{12,8},{16,12},{20,16},{24,20},{28,24},{1,29},{... | collective-permute-start | bytes 786440 | tf_op jit(solution)/shard_map/ppermute | solution.py:39
  57.4 12.1 %collective-permute-start.6 = (bf16[256,512]{1,0:T(8,128)(2,1)S(1)}, bf16[256,512]{1,0:T(8,128)(2,1)S(1)}, u32[]{:S(2)}, u32[]{:S(2)}) collective-permute-start(bf16[256,512]{1,0:T(8,128)(2,1)S(1)} %collective-permute-done.4), channel_id=1, source_target_pairs={{0,4},{4,8},{8,12},{12,16},{16,20},{20,24},{24,28},{28,0},{1,5},{5... | collective-permute-start | bytes 786440 | tf_op jit(solution)/shard_map/ppermute | solution.py:29
  72.6 1.0 copy-start.2
  169.0 3.0 %copy-start.4 = (f32[512,32]{0,1:T(8,128)S(1)}, f32[512,32]{0,1:T(8,128)}, u32[]{:S(2)}) copy-start(f32[512,32]{0,1:T(8,128)} %get-tuple-element.16) | copy-start | bytes 196612
  173.3 8.2 %copy-start.9 = (bf16[512,512]{0,1:T(8,128)(2,1)S(1)}, bf16[512,512]{0,1:T(8,128)(2,1)}, u32[]{:S(2)}) copy-start(bf16[512,512]{0,1:T(8,128)(2,1)} %fusion.11) | copy-start | bytes 1572868
Sparse Core Ops, SparseCore 0:
  9.5 58.7 all-gather.11
  70.4 48.5 all-gather.5
  121.2 47.7 all-gather.7
  170.9 49.5 all-gather.9
  224.8 29.5 reduce-scatter.1
